TPU v7x, 32 devices: a whole 2x2x4 slice. The times are simulated.
32 devices in a mesh: dp: 8 (over z, x), mp: 4 (over y, core).
Axes of the slice: x: 2, y: 2, z: 4, core: 2. Of those that a mesh axis runs over, the one named last changes fastest.
Arguments:
- tokens: bfloat16 [16, 1024, 1024], P('dp', 'mp'), may hold values from -6 to 6
- lengths: int32 [16], P('dp'), may hold values from 256 to 1024, as said below
- attn_norm: bfloat16 [1024], P('dp'), may hold values from 0.099609375 to 1.8984375
- qkv_weight: bfloat16 [3, 1024, 1024], P(None, 'dp', 'mp'), may hold values from -0.25 to 0.25
- attn_out_weight: bfloat16 [1024, 1024], P('mp', 'dp'), may hold values from -1.5 to 1.5
- ffn_norm: bfloat16 [1024], P('dp'), may hold values from 0.099609375 to 1.8984375
- ffn_in_weight: bfloat16 [2, 1024, 2624], P(None, 'dp', 'mp'), may hold values from -0.1875 to 0.1875
- ffn_out_weight: bfloat16 [2624, 1024], P('mp', 'dp'), may hold values from -0.125 to 0.125
- out_grad: bfloat16 [16, 1024, 1024], P('dp', 'mp'), may hold values from -6 to 6
Outputs:
- output: bfloat16 [16, 1024, 1024], P('dp', 'mp')
- grad_input: bfloat16 [16, 1024, 1024], P('dp', 'mp')
- grad_attn_norm: float32 [1024], P('dp')
- grad_qkv: float32 [3, 1024, 1024], P(None, 'dp', 'mp')
- grad_attn_out: float32 [1024, 1024], P('mp', 'dp')
- grad_ffn_norm: float32 [1024], P('dp')
- grad_ffn_in: float32 [2, 1024, 2624], P(None, 'dp', 'mp')
- grad_ffn_out: float32 [2624, 1024], P('mp', 'dp')
Inputs may be any that keep to these rules, and one draw needn't show every extreme that they name: Sequence s holds valid tokens at positions 0 to lengths[s] - 1 and padding after; some sequence has exactly 1024 and some exactly 256.
All inputs are finite; a program needn't handle non-finite values.
Results may differ from a plain program's by a relative error of at most 0.02.
Values may be sent and summed in bfloat16 or wider, within the bound.
No kernel may reach another device: no remote copies, remote signals or barrier semaphores. Data moves between devices by JAX's collectives and lax.ppermute only.
A program may use at most 192 MiB of HBM per device.

v0:
```python
import jax
import jax.numpy as jnp
from jax import lax
from jax.sharding import PartitionSpec as P

HD = 64
norm_eps = 1e-05
rope_base = 160000.0


def layer_norm(values, norm_gain):
    average = jnp.mean(values, axis=-1, keepdims=True)
    centred = values - average
    spread = jnp.mean(centred * centred, axis=-1, keepdims=True)
    return centred * lax.rsqrt(spread + norm_eps) * norm_gain


def rope_tables(length, head_size):
    places = jnp.arange(length, dtype=jnp.float32)
    frequency = rope_base ** (-jnp.arange(0, head_size, 2, dtype=jnp.float32) / head_size)
    angles = places[:, None] * frequency[None, :]
    angles = jnp.concatenate([angles, angles], axis=-1)
    return (jnp.cos(angles), jnp.sin(angles))


def rotate(values, cosine_table, sine_table):
    half_size = values.shape[-1] // 2
    turned = jnp.concatenate([-values[..., half_size:], values[..., :half_size]], axis=-1)
    return values * cosine_table + turned * sine_table


def unrotate(grad_rows, cosine_table, sine_table):
    half_size = grad_rows.shape[-1] // 2
    scaled = grad_rows * sine_table
    return grad_rows * cosine_table + jnp.concatenate(
        [scaled[..., half_size:], -scaled[..., :half_size]], axis=-1
    )


def gelu_product(up_rows, gate_rows):
    return jax.nn.gelu(up_rows, approximate=False) * gate_rows


def masked_scores(query_rows, key_rows, key_valid, score_scale):
    scores = (
        jnp.einsum("qhd,khd->hqk", query_rows, key_rows, preferred_element_type=jnp.float32)
        * score_scale
    )
    return jnp.where(key_valid[None, None, :], scores, -jnp.inf)


def fetch_attention(qkv_weight, attn_out_weight, attn_norm):
    return (
        lax.all_gather(qkv_weight, "dp", axis=1, tiled=True),
        lax.all_gather(attn_out_weight, "dp", axis=1, tiled=True),
        lax.all_gather(attn_norm, "dp", axis=0, tiled=True),
    )


def fetch_feedforward(ffn_in_weight, ffn_out_weight, ffn_norm):
    return (
        lax.all_gather(ffn_in_weight, "dp", axis=1, tiled=True),
        lax.all_gather(ffn_out_weight, "dp", axis=1, tiled=True),
        lax.all_gather(ffn_norm, "dp", axis=0, tiled=True),
    )


def fetch_attention_again(qkv_weight, attn_out_weight, attn_norm):
    return (
        lax.all_gather(qkv_weight, "dp", axis=1, tiled=True),
        lax.all_gather(attn_out_weight, "dp", axis=1, tiled=True),
        lax.all_gather(attn_norm, "dp", axis=0, tiled=True),
    )


def fetch_feedforward_again(ffn_in_weight, ffn_out_weight, ffn_norm):
    return (
        lax.all_gather(ffn_in_weight, "dp", axis=1, tiled=True),
        lax.all_gather(ffn_out_weight, "dp", axis=1, tiled=True),
        lax.all_gather(ffn_norm, "dp", axis=0, tiled=True),
    )


def per_device(
    tokens,
    lengths,
    attn_norm,
    qkv_weight,
    attn_out_weight,
    ffn_norm,
    ffn_in_weight,
    ffn_out_weight,
    out_grad,
):
    micro_count = tokens.shape[0]
    local_len = tokens.shape[1]
    width = tokens.shape[2]
    full_len = local_len * lax.axis_size("mp")
    head_cols = qkv_weight.shape[2]
    heads_dev = head_cols // HD
    units_dev = ffn_in_weight.shape[2]
    score_scale = HD ** (-0.5)
    offset = lax.axis_index("mp") * local_len
    positions = jnp.arange(full_len, dtype=jnp.int32)
    local_positions = offset + jnp.arange(local_len, dtype=jnp.int32)
    cosine_table, sine_table = rope_tables(full_len, HD)
    cosine_table = cosine_table[:, None, :]
    sine_table = sine_table[:, None, :]
    grad_qkv = jnp.zeros((3, width, head_cols), jnp.float32)
    grad_attn_out = jnp.zeros((head_cols, width), jnp.float32)
    grad_ffn_in = jnp.zeros((2, width, units_dev), jnp.float32)
    grad_ffn_out = jnp.zeros((units_dev, width), jnp.float32)
    grad_attn_gain = jnp.zeros((width,), jnp.float32)
    grad_ffn_gain = jnp.zeros((width,), jnp.float32)
    outputs = []
    input_grads = []
    for micro_step in range(micro_count):
        qkv_full, attn_out_full, attn_gain_low = fetch_attention(
            qkv_weight, attn_out_weight, attn_norm
        )
        ffn_in_full, ffn_out_full, ffn_gain_low = fetch_feedforward(
            ffn_in_weight, ffn_out_weight, ffn_norm
        )
        attn_gain = attn_gain_low.astype(jnp.float32)
        ffn_gain = ffn_gain_low.astype(jnp.float32)
        token_rows = tokens[micro_step].astype(jnp.float32)
        seq_length = lengths[micro_step]
        row_valid = (local_positions < seq_length).astype(jnp.float32)[:, None]
        key_valid = positions < seq_length
        normed_value, first_pull = jax.vjp(layer_norm, token_rows, attn_gain)
        normed_one = normed_value.astype(jnp.bfloat16)
        full_one = lax.all_gather(normed_one, "mp", axis=0, tiled=True)
        projected = jnp.einsum(
            "ld,cde->cle", full_one, qkv_full, preferred_element_type=jnp.float32
        )
        query_rows = rotate(
            projected[0].reshape(full_len, heads_dev, HD), cosine_table, sine_table
        ).astype(jnp.bfloat16)
        key_rows = rotate(
            projected[1].reshape(full_len, heads_dev, HD), cosine_table, sine_table
        ).astype(jnp.bfloat16)
        value_rows = projected[2].reshape(full_len, heads_dev, HD).astype(jnp.bfloat16)
        scores = masked_scores(query_rows, key_rows, key_valid, score_scale)
        top_score = jnp.max(scores, axis=-1, keepdims=True)
        log_total = top_score + jnp.log(
            jnp.sum(jnp.exp(scores - top_score), axis=-1, keepdims=True)
        )
        probabilities = jnp.exp(scores - log_total).astype(jnp.bfloat16)
        context = jnp.einsum(
            "hqk,khd->qhd", probabilities, value_rows, preferred_element_type=jnp.float32
        )
        context = context.astype(jnp.bfloat16).reshape(full_len, head_cols)
        attention = lax.psum_scatter(
            jnp.dot(context, attn_out_full, preferred_element_type=jnp.float32),
            "mp",
            scatter_dimension=0,
            tiled=True,
        )
        hidden = token_rows + attention
        normed_hidden, second_pull = jax.vjp(layer_norm, hidden, ffn_gain)
        normed_two = normed_hidden.astype(jnp.bfloat16)
        full_two = lax.all_gather(normed_two, "mp", axis=0, tiled=True)
        up_gate = jnp.einsum(
            "ld,cdf->clf", full_two, ffn_in_full, preferred_element_type=jnp.float32
        )
        mixed_value, gelu_pull = jax.vjp(gelu_product, up_gate[0], up_gate[1])
        mixed_rows = mixed_value.astype(jnp.bfloat16)
        feedforward = lax.psum_scatter(
            jnp.dot(mixed_rows, ffn_out_full, preferred_element_type=jnp.float32).astype(
                jnp.bfloat16
            ),
            "mp",
            scatter_dimension=0,
            tiled=True,
        ).astype(jnp.float32)
        outputs.append((row_valid * (hidden + feedforward)).astype(jnp.bfloat16))
        qkv_full, attn_out_full, attn_gain_low = fetch_attention_again(
            qkv_weight, attn_out_weight, attn_norm
        )
        ffn_in_full, ffn_out_full, ffn_gain_low = fetch_feedforward_again(
            ffn_in_weight, ffn_out_weight, ffn_norm
        )
        out_back = row_valid * out_grad[micro_step].astype(jnp.float32)
        full_out_back = lax.all_gather(out_back.astype(jnp.bfloat16), "mp", axis=0, tiled=True)
        grad_ffn_out = grad_ffn_out + jnp.einsum(
            "lf,ld->fd", mixed_rows, full_out_back, preferred_element_type=jnp.float32
        )
        mixed_back = jnp.einsum(
            "ld,fd->lf", full_out_back, ffn_out_full, preferred_element_type=jnp.float32
        )
        up_back, gate_back = gelu_pull(mixed_back)
        up_gate_back = jnp.stack([up_back, gate_back]).astype(jnp.bfloat16)
        grad_ffn_in = grad_ffn_in + jnp.einsum(
            "ld,clf->cdf", full_two, up_gate_back, preferred_element_type=jnp.float32
        )
        normed_two_back = lax.psum_scatter(
            jnp.einsum(
                "clf,cdf->ld", up_gate_back, ffn_in_full, preferred_element_type=jnp.float32
            ).astype(jnp.bfloat16),
            "mp",
            scatter_dimension=0,
            tiled=True,
        ).astype(jnp.float32)
        hidden_norm_back, ffn_gain_part = second_pull(normed_two_back)
        grad_ffn_gain = grad_ffn_gain + ffn_gain_part
        hidden_back = out_back + hidden_norm_back
        full_hidden_back = lax.all_gather(
            hidden_back.astype(jnp.bfloat16), "mp", axis=0, tiled=True
        )
        grad_attn_out = grad_attn_out + jnp.einsum(
            "le,ld->ed", context, full_hidden_back, preferred_element_type=jnp.float32
        )
        context_back = jnp.einsum(
            "ld,ed->le", full_hidden_back, attn_out_full, preferred_element_type=jnp.float32
        )
        context_back = context_back.astype(jnp.bfloat16).reshape(full_len, heads_dev, HD)
        scores_again = masked_scores(query_rows, key_rows, key_valid, score_scale)
        probs_again = jnp.exp(scores_again - log_total)
        value_back = jnp.einsum(
            "hqk,qhd->khd",
            probs_again.astype(jnp.bfloat16),
            context_back,
            preferred_element_type=jnp.float32,
        )
        probs_back = jnp.einsum(
            "qhd,khd->hqk", context_back, value_rows, preferred_element_type=jnp.float32
        )
        row_inner = jnp.sum(probs_again * probs_back, axis=-1, keepdims=True)
        scores_back = (probs_again * (probs_back - row_inner)).astype(jnp.bfloat16)
        query_grad = (
            jnp.einsum("hqk,khd->qhd", scores_back, key_rows, preferred_element_type=jnp.float32)
            * score_scale
        )
        key_grad = (
            jnp.einsum("hqk,qhd->khd", scores_back, query_rows, preferred_element_type=jnp.float32)
            * score_scale
        )
        query_back = unrotate(query_grad, cosine_table, sine_table).astype(jnp.bfloat16)
        key_back = unrotate(key_grad, cosine_table, sine_table).astype(jnp.bfloat16)
        projected_back = jnp.stack(
            [
                query_back.reshape(full_len, head_cols),
                key_back.reshape(full_len, head_cols),
                value_back.astype(jnp.bfloat16).reshape(full_len, head_cols),
            ]
        )
        grad_qkv = grad_qkv + jnp.einsum(
            "ld,cle->cde", full_one, projected_back, preferred_element_type=jnp.float32
        )
        normed_one_back = lax.psum_scatter(
            jnp.einsum(
                "cle,cde->ld", projected_back, qkv_full, preferred_element_type=jnp.float32
            ).astype(jnp.bfloat16),
            "mp",
            scatter_dimension=0,
            tiled=True,
        ).astype(jnp.float32)
        token_back, attn_gain_part = first_pull(normed_one_back)
        grad_attn_gain = grad_attn_gain + attn_gain_part
        input_grads.append((hidden_back + token_back).astype(jnp.bfloat16))
    shards = (
        lax.psum_scatter(
            grad_qkv.astype(jnp.bfloat16), "dp", scatter_dimension=1, tiled=True
        ).astype(jnp.float32),
        lax.psum_scatter(
            grad_attn_out.astype(jnp.bfloat16), "dp", scatter_dimension=1, tiled=True
        ).astype(jnp.float32),
        lax.psum_scatter(
            grad_ffn_in.astype(jnp.bfloat16), "dp", scatter_dimension=1, tiled=True
        ).astype(jnp.float32),
        lax.psum_scatter(
            grad_ffn_out.astype(jnp.bfloat16), "dp", scatter_dimension=1, tiled=True
        ).astype(jnp.float32),
        lax.psum_scatter(
            grad_attn_gain.astype(jnp.bfloat16), "dp", scatter_dimension=0, tiled=True
        ).astype(jnp.float32),
        lax.psum_scatter(
            grad_ffn_gain.astype(jnp.bfloat16), "dp", scatter_dimension=0, tiled=True
        ).astype(jnp.float32),
    )
    attn_gain_total, ffn_gain_total = lax.psum((shards[4], shards[5]), "mp")
    return (
        jnp.stack(outputs),
        jnp.stack(input_grads),
        attn_gain_total,
        shards[0],
        shards[1],
        ffn_gain_total,
        shards[2],
        shards[3],
    )


def solution(mesh):
    in_specs = (
        P("dp", "mp", None),
        P("dp"),
        P("dp"),
        P(None, "dp", "mp"),
        P("mp", "dp"),
        P("dp"),
        P(None, "dp", "mp"),
        P("mp", "dp"),
        P("dp", "mp", None),
    )
    out_specs = (
        P("dp", "mp", None),
        P("dp", "mp", None),
        P("dp"),
        P(None, "dp", "mp"),
        P("mp", "dp"),
        P("dp"),
        P(None, "dp", "mp"),
        P("mp", "dp"),
    )
    return jax.shard_map(
        per_device, mesh=mesh, in_specs=in_specs, out_specs=out_specs, check_vma=False
    )
```

profile of v0, /device:TPU:0, one launch (start us, length us, event | category | flops | bytes accessed | tf_op | source)
XLA Modules:
  0.0 1003.6 jit_solution(15254512548151848023)
XLA Ops:
  9.1 22.3 %all-gather = bf16[8,1,128]{2,1,0:T(2,128)(2,1)S(1)} all-gather(bf16[1,1,128]{2,1,0:T(2,128)(2,1)} %bitcast.478), channel_id=1, replica_groups=mesh['dp'=8,'mp'=4] {'dp'}, dimensions={0}, use_global_device_ids=true | all-gather | bytes 2304 | tf_op jit(solution)/shard_map/all_gather | solution.py:56
  40.3 30.8 %all_gather.59 = bf16[256,1024]{1,0:T(8,128)(2,1)} all-gather(bf16[256,128]{1,0:T(8,128)(2,1)S(1)} %copy-done.60), channel_id=1, replica_groups=mesh['dp'=8,'mp'=4] {'dp'}, dimensions={1}, use_global_device_ids=true | all-gather | bytes 589824 | tf_op jit(solution)/shard_map/all_gather | solution.py:55
  71.1 16.6 %all-gather.14.cloned.1.call-done = bf16[1024,1024]{1,0:T(8,128)(2,1)} async-done(((bf16[256,1024]{1,0:T(8,128)(2,1)}), bf16[1024,1024]{1,0:T(8,128)(2,1)}) %all-gather.14.cloned.1.call-update) | async-done | bytes 2097168 | tf_op jit(solution)/shard_map/all_gather | solution.py:132
  92.7 19.8 %all-gather.24.cloned.1.call-done = bf16[1024,1024]{1,0:T(8,128)(2,1)} async-done(((bf16[256,1024]{1,0:T(8,128)(2,1)}), bf16[1024,1024]{1,0:T(8,128)(2,1)}) %all-gather.24.cloned.1.call-update) | async-done | bytes 2097168 | tf_op jit(solution)/shard_map/all_gather | solution.py:132
  168.0 20.9 %all-gather.1 = bf16[8,1,128]{2,1,0:T(2,128)(2,1)S(1)} all-gather(bf16[1,1,128]{2,1,0:T(2,128)(2,1)S(1)} %bitcast.479), channel_id=1, replica_groups=mesh['dp'=8,'mp'=4] {'dp'}, dimensions={0}, use_global_device_ids=true | all-gather | bytes 2304 | tf_op jit(solution)/shard_map/all_gather | solution.py:64
  188.9 43.7 %reduce-scatter.25.cloned.1.call-done = f32[256,1024]{1,0:T(8,128)} async-done(((f32[1024,1024]{1,0:T(8,128)}), f32[256,1024]{1,0:T(8,128)}) %reduce-scatter.25.cloned.1.call-update) | async-done | bytes 1048592 | tf_op jit(solution)/shard_map/reduce_scatter | solution.py:153
  236.9 40.2 %all-gather.22.cloned.1.call-done = bf16[656,1024]{1,0:T(8,128)(2,1)} async-done(((bf16[656,128]{1,0:T(8,128)(2,1)}), bf16[656,1024]{1,0:T(8,128)(2,1)}) %all-gather.22.cloned.1.call-update) | async-done | bytes 1343504 | tf_op jit(solution)/shard_map/all_gather | solution.py:63
  277.1 23.4 %all-gather.32.cloned.1.call-done = bf16[1024,1024]{1,0:T(8,128)(2,1)} async-done(((bf16[256,1024]{1,0:T(8,128)(2,1)}), bf16[1024,1024]{1,0:T(8,128)(2,1)}) %all-gather.32.cloned.1.call-update) | async-done | bytes 2097168 | tf_op jit(solution)/shard_map/all_gather | solution.py:184
  305.7 54.5 %all-gather.20.cloned.1.call-done = bf16[2,1024,656]{1,2,0:T(8,128)(2,1)} async-done(((bf16[2,128,656]{1,2,0:T(8,128)(2,1)}), bf16[2,1024,656]{1,2,0:T(8,128)(2,1)}) %all-gather.20.cloned.1.call-update) | async-done | bytes 2686992 | tf_op jit(solution)/shard_map/all_gather | solution.py:62
  360.2 22.4 %all-gather.26.cloned.1.call-done = bf16[1024,1024]{1,0:T(8,128)(2,1)} async-done(((bf16[256,1024]{1,0:T(8,128)(2,1)}), bf16[1024,1024]{1,0:T(8,128)(2,1)}) %all-gather.26.cloned.1.call-update) | async-done | bytes 2097168 | tf_op jit(solution)/shard_map/all_gather | solution.py:162
  412.3 19.1 %all-gather.18.cloned.1.call-done = bf16[1024,1024]{1,0:T(8,128)(2,1)} async-done(((bf16[256,1024]{1,0:T(8,128)(2,1)}), bf16[1024,1024]{1,0:T(8,128)(2,1)}) %all-gather.18.cloned.1.call-update) | async-done | bytes 2097168 | tf_op jit(solution)/shard_map/all_gather | solution.py:162
  465.2 34.1 %reduce-scatter.29.cloned.1.call-done = bf16[256,1024]{1,0:T(8,128)(2,1)} async-done(((bf16[1024,1024]{1,0:T(8,128)(2,1)}), bf16[256,1024]{1,0:T(8,128)(2,1)}) %reduce-scatter.29.cloned.1.call-update) | async-done | bytes 524304 | tf_op jit(solution)/shard_map/reduce_scatter | solution.py:196
  502.0 31.2 %reduce-scatter.27.cloned.1.call-done = bf16[256,1024]{1,0:T(8,128)(2,1)} async-done(((bf16[1024,1024]{1,0:T(8,128)(2,1)}), bf16[256,1024]{1,0:T(8,128)(2,1)}) %reduce-scatter.27.cloned.1.call-update) | async-done | bytes 524304 | tf_op jit(solution)/shard_map/reduce_scatter | solution.py:168
  533.2 34.0 %reduce-scatter.23.cloned.1.call-done = bf16[256,1024]{1,0:T(8,128)(2,1)} async-done(((bf16[1024,1024]{1,0:T(8,128)(2,1)}), bf16[256,1024]{1,0:T(8,128)(2,1)}) %reduce-scatter.23.cloned.1.call-update) | async-done | bytes 524304 | tf_op jit(solution)/shard_map/reduce_scatter | solution.py:168
  604.5 14.8 %multiply_reduce_fusion.1 = (f32[4,1024]{1,0:T(4,128)S(1)}, f32[4,1024,1024]{1,2,0:T(8,128)}) fusion(f32[4,1024,1024]{1,2,0:T(8,128)} %copy-done.1, f32[4,1024]{1,0:T(4,128)S(1)} %log_add_fusion.1, pred[1024]{0:T(1024)(128)(4,1)S(1)} %iota_compare_fusion.1, bf16[1024,4,64]{0,2,1:T(8,128)(2,1)S(1)} %bitcast.455, bf16[1024,4,64]{0,2,1:T(8,128)(2,1)S(1)} %bitcast.452), kind=kOutput, calls=%fused_computation.3 | convolution fusion | flops 557838336 | bytes 34636800 | tf_op jit(solution)/shard_map/qhd,khd->hqk/dot_general | solution.py:225
  621.1 8.6 multiply_convert_fusion.1
  642.8 15.3 %multiply_reduce_fusion = (f32[4,1024]{1,0:T(4,128)}, f32[4,1024,1024]{1,2,0:T(8,128)}) fusion(f32[4,1024,1024]{1,2,0:T(8,128)} %copy-done, f32[4,1024]{1,0:T(4,128)S(1)} %log_add_fusion, pred[1024]{0:T(1024)(128)(4,1)S(1)} %iota_compare_fusion, bf16[1024,4,64]{0,2,1:T(8,128)(2,1)} %bitcast.457, bf16[1024,4,64]{0,2,1:T(8,128)(2,1)S(1)} %bitcast.454), kind=kOutput, calls=%fused_computation.1 | convolution fusion | flops 557838336 | bytes 34636800 | tf_op jit(solution)/shard_map/qhd,khd->hqk/dot_general | solution.py:225
  659.6 9.1 multiply_convert_fusion
  717.9 44.1 %reduce-scatter.41.cloned.1.call-done = bf16[128,1312]{1,0:T(8,128)(2,1)} async-done(((bf16[1024,1312]{1,0:T(8,128)(2,1)}), bf16[128,1312]{1,0:T(8,128)(2,1)}) %reduce-scatter.41.cloned.1.call-update) | async-done | bytes 335888
  765.0 61.6 %reduce-scatter.39.cloned.1.call-done = bf16[128,256]{1,0:T(8,128)(2,1)} async-done(((bf16[1024,256]{1,0:T(8,128)(2,1)}), bf16[128,256]{1,0:T(8,128)(2,1)}) %reduce-scatter.39.cloned.1.call-update) | async-done | bytes 65552
  828.3 65.6 %reduce-scatter.37.cloned.1.call-done = bf16[128,768]{1,0:T(8,128)(2,1)} async-done(((bf16[1024,768]{1,0:T(8,128)(2,1)}), bf16[128,768]{1,0:T(8,128)(2,1)}) %reduce-scatter.37.cloned.1.call-update) | async-done | bytes 196624
  896.1 30.9 %reduce-scatter.35.cloned.1.call-done = bf16[256,1024]{1,0:T(8,128)(2,1)} async-done(((bf16[1024,1024]{1,0:T(8,128)(2,1)}), bf16[256,1024]{1,0:T(8,128)(2,1)}) %reduce-scatter.35.cloned.1.call-update) | async-done | bytes 524304 | tf_op jit(solution)/shard_map/reduce_scatter | solution.py:250
  927.0 34.0 %reduce-scatter.31.cloned.1.call-done = bf16[256,1024]{1,0:T(8,128)(2,1)} async-done(((bf16[1024,1024]{1,0:T(8,128)(2,1)}), bf16[256,1024]{1,0:T(8,128)(2,1)}) %reduce-scatter.31.cloned.1.call-update) | async-done | bytes 524304 | tf_op jit(solution)/shard_map/reduce_scatter | solution.py:250
  965.2 21.4 %all-reduce.3 = (bf16[1024]{0:T(1024)(128)(2,1)S(1)}, bf16[1024]{0:T(1024)(128)(2,1)S(1)}) all-reduce(bf16[1024]{0:T(1024)(128)(2,1)S(1)} %add_convert_fusion.6, bf16[1024]{0:T(1024)(128)(2,1)S(1)} %add_convert_fusion.5), channel_id=10, replica_groups=mesh['dp'=8,'mp'=4] {'dp'}, use_global_device_ids=true, to_apply=%region_32.33.clone | all-reduce | flops 2048 | bytes 8192
  (389 shorter events, 268.8 us)
Async XLA Ops:
  7.2 64.0 %all-gather.16.cloned.1.call-start = ((), (), s32[]{:S(2)}) async-start(), calls=%async_computation.13 | async-start | bytes 1769472 | tf_op jit(solution)/shard_map/all_gather | solution.py:54
  9.1 78.7 %all-gather.14.cloned.1.call-start = ((), (), s32[]{:S(2)}) async-start(), calls=%async_computation.12 | async-start | bytes 2621440 | tf_op jit(solution)/shard_map/all_gather | solution.py:132
  36.5 76.1 %all-gather.24.cloned.1.call-start = ((), (), s32[]{:S(2)}) async-start(), calls=%async_computation.19 | async-start | bytes 2621440 | tf_op jit(solution)/shard_map/all_gather | solution.py:132
  37.2 151.7 %reduce-scatter.21.cloned.1.call-start = ((), (), s32[]{:S(2)}) async-start(), calls=%async_computation.14 | async-start | bytes 5242880 | tf_op jit(solution)/shard_map/reduce_scatter | solution.py:153
  140.8 91.7 %reduce-scatter.25.cloned.1.call-start = ((), (), s32[]{:S(2)}) async-start(), calls=%async_computation.20 | async-start | bytes 5242880 | tf_op jit(solution)/shard_map/reduce_scatter | solution.py:153
  164.0 113.1 %all-gather.22.cloned.1.call-start = ((), (), s32[]{:S(2)}) async-start(), calls=%async_computation.17 | async-start | bytes 1511424 | tf_op jit(solution)/shard_map/all_gather | solution.py:63
  164.6 135.9 %all-gather.32.cloned.1.call-start = ((), (), s32[]{:S(2)}) async-start(), calls=%async_computation.27 | async-start | bytes 2621440 | tf_op jit(solution)/shard_map/all_gather | solution.py:184
  165.9 404.6 %copy-start.65 = (f32[256]{0:T(256)}, f32[256]{0:T(256)S(1)}, u32[]{:S(2)}) copy-start(f32[256]{0:T(256)S(1)} %get-tuple-element.125) | copy-start | bytes 3076
  167.2 193.0 %all-gather.20.cloned.1.call-start = ((), (), s32[]{:S(2)}) async-start(), calls=%async_computation.16 | async-start | bytes 3022848 | tf_op jit(solution)/shard_map/all_gather | solution.py:62
  167.9 214.7 %all-gather.26.cloned.1.call-start = ((), (), s32[]{:S(2)}) async-start(), calls=%async_computation.21 | async-start | bytes 2621440 | tf_op jit(solution)/shard_map/all_gather | solution.py:162
  236.3 170.9 %all-gather.28.cloned.1.call-start = ((), (), s32[]{:S(2)}) async-start(), calls=%async_computation.23 | async-start | bytes 2621440 | tf_op jit(solution)/shard_map/all_gather | solution.py:184
  236.9 194.5 %all-gather.18.cloned.1.call-start = ((), (), s32[]{:S(2)}) async-start(), calls=%async_computation.15 | async-start | bytes 2621440 | tf_op jit(solution)/shard_map/all_gather | solution.py:162
  305.6 159.6 %reduce-scatter.33.cloned.1.call-start = ((), (), s32[]{:S(2)}) async-start(), calls=%async_computation.28 | async-start | bytes 2621440 | tf_op jit(solution)/shard_map/reduce_scatter | solution.py:196
  403.0 96.4 %reduce-scatter.29.cloned.1.call-start = ((), (), s32[]{:S(2)}) async-start(), calls=%async_computation.24 | async-start | bytes 2621440 | tf_op jit(solution)/shard_map/reduce_scatter | solution.py:196
  451.7 81.5 %reduce-scatter.27.cloned.1.call-start = ((), (), s32[]{:S(2)}) async-start(), calls=%async_computation.22 | async-start | bytes 2621440 | tf_op jit(solution)/shard_map/reduce_scatter | solution.py:168
  456.7 110.5 %reduce-scatter.23.cloned.1.call-start = ((), (), s32[]{:S(2)}) async-start(), calls=%async_computation.18 | async-start | bytes 2621440 | tf_op jit(solution)/shard_map/reduce_scatter | solution.py:168
  461.7 139.3 %all-gather.30.cloned.1.call-start = ((), (), s32[]{:S(2)}) async-start(), calls=%async_computation.25 | async-start | bytes 2621440 | tf_op jit(solution)/shard_map/all_gather | solution.py:207
  572.2 63.7 %all-gather.34.cloned.1.call-start = ((), (), s32[]{:S(2)}) async-start(), calls=%async_computation.29 | async-start | bytes 2621440 | tf_op jit(solution)/shard_map/all_gather | solution.py:207
  572.8 142.1 %reduce-scatter.43.cloned.1.call-start = ((), (), s32[]{:S(2)}) async-start(), calls=%async_computation.34 | async-start | bytes 1769472
  579.4 182.6 %reduce-scatter.41.cloned.1.call-start = ((), (), s32[]{:S(2)}) async-start(), calls=%async_computation.33 | async-start | bytes 3244032
  601.0 225.7 %reduce-scatter.39.cloned.1.call-start = ((), (), s32[]{:S(2)}) async-start(), calls=%async_computation.32 | async-start | bytes 589824
  684.1 209.8 %reduce-scatter.37.cloned.1.call-start = ((), (), s32[]{:S(2)}) async-start(), calls=%async_computation.31 | async-start | bytes 1769472
  705.0 222.0 %reduce-scatter.35.cloned.1.call-start = ((), (), s32[]{:S(2)}) async-start(), calls=%async_computation.30 | async-start | bytes 2621440 | tf_op jit(solution)/shard_map/reduce_scatter | solution.py:250
  710.2 250.7 %reduce-scatter.31.cloned.1.call-start = ((), (), s32[]{:S(2)}) async-start(), calls=%async_computation.26 | async-start | bytes 2621440 | tf_op jit(solution)/shard_map/reduce_scatter | solution.py:250
  (101 other events, 2683.0 us)
Sparse Core Ops, SparseCore 0:
  10.6 51.3 all-gather.15
  64.2 23.5 all-gather.13
  89.9 22.5 all-gather.23
  141.0 44.5 reduce-scatter.20
  188.1 44.4 reduce-scatter.24
  234.5 42.5 all-gather.21
  279.3 21.2 all-gather.31
  302.5 57.6 all-gather.19
  361.8 20.7 all-gather.25
  384.6 22.5 all-gather.27
  408.8 22.5 all-gather.17
  433.8 31.4 reduce-scatter.32
  467.9 31.3 reduce-scatter.28
  501.7 31.4 reduce-scatter.26
  535.7 31.3 reduce-scatter.22
  572.3 22.6 all-gather.29
  596.4 22.5 all-gather.33
  622.3 64.7 reduce-scatter.42
  691.1 70.9 reduce-scatter.40
  765.6 61.0 reduce-scatter.38
  830.1 63.7 reduce-scatter.36
  896.6 30.3 reduce-scatter.34
  929.5 31.3 reduce-scatter.30
where the time goes:
time: 1010 us; the launch traced here: 1000 us
  waiting for transfers between devices  586 us (58%)
  matrix products  149 us (15%)
  blocking collectives  102 us (10%)
  other arithmetic  96 us (10%)
  local copies, waits for them, and re-layouts  53.1 us (5%)
  between operations  16.4 us (2%)
    unnamed x27, waiting for transfers between devices  175 us
    reduce_scatter x2, waiting for transfers between devices, per_device(): lax.psum_scatter(jnp.dot(mixed_rows, ffn_out_full, preferred_element_type...  65.2 us
    reduce_scatter x2, waiting for transfers between devices, per_device(): lax.psum_scatter(jnp.einsum('cle,cde->ld', projected_back, qkv_full, pref...  64.9 us
    all_gather x1, waiting for transfers between devices, fetch_feedforward(): lax.all_gather(ffn_in_weight, 'dp', axis=1, tiled=True)  54.5 us
    unnamed x219, local copies, waits for them, and re-layouts  46.2 us
    reduce_scatter x2, waiting for transfers between devices, per_device(): lax.psum_scatter(jnp.dot(context, attn_out_full, preferred_element_type=j...  43.7 us
    all_gather x2, waiting for transfers between devices, per_device(): full_two = lax.all_gather(normed_two, 'mp', axis=0, tiled=True)  41.5 us
    all_gather x1, waiting for transfers between devices, fetch_feedforward(): lax.all_gather(ffn_out_weight, 'dp', axis=1, tiled=True)  40.2 us
  transfers between devices with their start and end apart: 23, of which 18 were waited for; matrix products, arithmetic and copies ran while one was open for 24% of the time, Pallas kernels for 0%

commit v1 on v0

--- a/solution.py
+++ b/solution.py
@@ -58,8 +58,22 @@
 
 
 def fetch_feedforward(ffn_in_weight, ffn_out_weight, ffn_norm):
-    return (
-        lax.all_gather(ffn_in_weight, "dp", axis=1, tiled=True),
+
+    def shards_write(frame_in, along_dim):
+        new = lax.psum(1, "dp")
+        heard = lax.axis_index("dp")
+        e_now, even = (new, heard)
+        arr_out, outer = (frame_in, 1)
+        while outer < e_now:
+            piece_now = lax.ppermute(arr_out, "dp", perm=[(dd, dd ^ outer) for dd in range(e_now)])
+            n_now = jnp.concatenate([arr_out, piece_now], axis=along_dim)
+            res = jnp.concatenate([piece_now, arr_out], axis=along_dim)
+            arr_out = jnp.where(even & outer == 0, n_now, res)
+            outer = 2 * outer
+        return arr_out
+
+    return (
+        shards_write(ffn_in_weight, 1),
         lax.all_gather(ffn_out_weight, "dp", axis=1, tiled=True),
         lax.all_gather(ffn_norm, "dp", axis=0, tiled=True),
     )

time: 1010 us -> 1050 us (1.040)
  waiting for transfers between devices: 586 us -> 598 us
    ppermute x0 -> x3, waiting for transfers between devices: none -> 31 us  [shards_write(): lax.ppermute(arr_out, 'dp', perm=[(dd, dd ^ outer) for dd in range(e_now)])]
    unnamed x27, waiting for transfers between devices: 175 us -> 162 us
    all_gather x2, waiting for transfers between devices: 27.2 us -> 38.7 us  [per_device(): lax.all_gather(out_back.astype(jnp.bfloat16), 'mp', axis=0, tiled=True)]
    all_gather x1, waiting for transfers between devices: 54.5 us -> 43.7 us  [fetch_feedforward_again(): lax.all_gather(ffn_in_weight, 'dp', axis=1, tiled=True)]
    unnamed x219 -> x225, local copies, waits for them, and re-layouts: 46.2 us -> 46.4 us
  transfers between devices with their start and end apart: 23 -> 26, of which waited for: 18 -> 20; matrix products, arithmetic and copies ran while one was open for 24% -> 25% of each run, Pallas kernels for 0% -> 0%
where the time goes in v1:
time: 1050 us; the launch traced here: 1040 us
  waiting for transfers between devices  598 us (57%)
  matrix products  159 us (15%)
  other arithmetic  103 us (10%)
  blocking collectives  102 us (10%)
  local copies, waits for them, and re-layouts  54.7 us (5%)
  between operations  16.5 us (2%)
    unnamed x27, waiting for transfers between devices  162 us
    reduce_scatter x2, waiting for transfers between devices, per_device(): lax.psum_scatter(jnp.dot(mixed_rows, ffn_out_full, preferred_element_type...  65.2 us
    reduce_scatter x2, waiting for transfers between devices, per_device(): lax.psum_scatter(jnp.einsum('cle,cde->ld', projected_back, qkv_full, pref...  64.9 us
    unnamed x225, local copies, waits for them, and re-layouts  46.4 us
    reduce_scatter x2, waiting for transfers between devices, per_device(): lax.psum_scatter(jnp.dot(context, attn_out_full, preferred_element_type=j...  44.4 us
    all_gather x1, waiting for transfers between devices, fetch_feedforward_again(): lax.all_gather(ffn_in_weight, 'dp', axis=1, tiled=True)  43.7 us
    all_gather x2, waiting for transfers between devices, per_device(): lax.all_gather(out_back.astype(jnp.bfloat16), 'mp', axis=0, tiled=True)  38.7 us
    all_gather x2, waiting for transfers between devices, per_device(): full_two = lax.all_gather(normed_two, 'mp', axis=0, tiled=True)  38.2 us
  transfers between devices with their start and end apart: 26, of which 20 were waited for; matrix products, arithmetic and copies ran while one was open for 25% of the time, Pallas kernels for 0%

profile of v1, /device:TPU:0, one launch (start us, length us, event | category | flops | bytes accessed | tf_op | source)
XLA Modules:
  0.0 1041.1 jit_solution(6290410844251133537)
XLA Ops:
  9.1 22.3 %all-gather = bf16[8,1,128]{2,1,0:T(2,128)(2,1)S(1)} all-gather(bf16[1,1,128]{2,1,0:T(2,128)(2,1)} %bitcast.476), channel_id=1, replica_groups=mesh['dp'=8,'mp'=4] {'dp'}, dimensions={0}, use_global_device_ids=true | all-gather | bytes 2304 | tf_op jit(solution)/shard_map/all_gather | solution.py:56
  40.4 30.7 %all_gather.57 = bf16[256,1024]{1,0:T(8,128)(2,1)} all-gather(bf16[256,128]{1,0:T(8,128)(2,1)S(1)} %copy-done.62), channel_id=1, replica_groups=mesh['dp'=8,'mp'=4] {'dp'}, dimensions={1}, use_global_device_ids=true | all-gather | bytes 589824 | tf_op jit(solution)/shard_map/all_gather | solution.py:55
  71.2 16.4 %all-gather.22.cloned.1.call-done = bf16[1024,1024]{1,0:T(8,128)(2,1)} async-done(((bf16[256,1024]{1,0:T(8,128)(2,1)}), bf16[1024,1024]{1,0:T(8,128)(2,1)}) %all-gather.22.cloned.1.call-update) | async-done | bytes 2097168 | tf_op jit(solution)/shard_map/all_gather | solution.py:146
  92.6 19.8 %all-gather.14.cloned.1.call-done = bf16[1024,1024]{1,0:T(8,128)(2,1)} async-done(((bf16[256,1024]{1,0:T(8,128)(2,1)}), bf16[1024,1024]{1,0:T(8,128)(2,1)}) %all-gather.14.cloned.1.call-update) | async-done | bytes 2097168 | tf_op jit(solution)/shard_map/all_gather | solution.py:146
  167.2 20.9 %all-gather.1 = bf16[8,1,128]{2,1,0:T(2,128)(2,1)S(1)} all-gather(bf16[1,1,128]{2,1,0:T(2,128)(2,1)S(1)} %bitcast.477), channel_id=1, replica_groups=mesh['dp'=8,'mp'=4] {'dp'}, dimensions={0}, use_global_device_ids=true | all-gather | bytes 2304 | tf_op jit(solution)/shard_map/all_gather | solution.py:78
  188.1 44.4 %reduce-scatter.21.cloned.1.call-done = f32[256,1024]{1,0:T(8,128)} async-done(((f32[1024,1024]{1,0:T(8,128)}), f32[256,1024]{1,0:T(8,128)}) %reduce-scatter.21.cloned.1.call-update) | async-done | bytes 1048592 | tf_op jit(solution)/shard_map/reduce_scatter | solution.py:167
  250.8 21.1 %collective-permute-done.1 = bf16[2,256,656]{1,2,0:T(8,128)(2,1)} collective-permute-done((bf16[2,256,656]{1,2,0:T(8,128)(2,1)S(1)}, bf16[2,256,656]{1,2,0:T(8,128)(2,1)}, u32[]{:S(2)}, u32[]{:S(2)}) %collective-permute-start.1) | collective-permute-done | bytes 671776 | tf_op jit(solution)/shard_map/ppermute | solution.py:68
  277.7 36.4 %all-gather.20.cloned.1.call-done = bf16[656,1024]{1,0:T(8,128)(2,1)} async-done(((bf16[656,128]{1,0:T(8,128)(2,1)}), bf16[656,1024]{1,0:T(8,128)(2,1)}) %all-gather.20.cloned.1.call-update) | async-done | bytes 1343504 | tf_op jit(solution)/shard_map/all_gather | solution.py:77
  314.1 23.7 %all-gather.26.cloned.1.call-done = bf16[1024,1024]{1,0:T(8,128)(2,1)} async-done(((bf16[256,1024]{1,0:T(8,128)(2,1)}), bf16[1024,1024]{1,0:T(8,128)(2,1)}) %all-gather.26.cloned.1.call-update) | async-done | bytes 2097168 | tf_op jit(solution)/shard_map/all_gather | solution.py:198
  343.0 19.0 %all-gather.18.cloned.1.call-done = bf16[1024,1024]{1,0:T(8,128)(2,1)} async-done(((bf16[256,1024]{1,0:T(8,128)(2,1)}), bf16[1024,1024]{1,0:T(8,128)(2,1)}) %all-gather.18.cloned.1.call-update) | async-done | bytes 2097168 | tf_op jit(solution)/shard_map/all_gather | solution.py:176
  378.0 43.7 %all-gather.28.cloned.1.call-done = bf16[2,1024,656]{1,2,0:T(8,128)(2,1)} async-done(((bf16[2,128,656]{1,2,0:T(8,128)(2,1)}), bf16[2,1024,656]{1,2,0:T(8,128)(2,1)}) %all-gather.28.cloned.1.call-update) | async-done | bytes 2686992 | tf_op jit(solution)/shard_map/all_gather | solution.py:92
  429.6 15.0 %all-gather.32.cloned.1.call-done = bf16[1024,1024]{1,0:T(8,128)(2,1)} async-done(((bf16[256,1024]{1,0:T(8,128)(2,1)}), bf16[1024,1024]{1,0:T(8,128)(2,1)}) %all-gather.32.cloned.1.call-update) | async-done | bytes 2097168 | tf_op jit(solution)/shard_map/all_gather | solution.py:198
  449.6 19.1 %all-gather.24.cloned.1.call-done = bf16[1024,1024]{1,0:T(8,128)(2,1)} async-done(((bf16[256,1024]{1,0:T(8,128)(2,1)}), bf16[1024,1024]{1,0:T(8,128)(2,1)}) %all-gather.24.cloned.1.call-update) | async-done | bytes 2097168 | tf_op jit(solution)/shard_map/all_gather | solution.py:176
  502.6 34.1 %reduce-scatter.33.cloned.1.call-done = bf16[256,1024]{1,0:T(8,128)(2,1)} async-done(((bf16[1024,1024]{1,0:T(8,128)(2,1)}), bf16[256,1024]{1,0:T(8,128)(2,1)}) %reduce-scatter.33.cloned.1.call-update) | async-done | bytes 524304 | tf_op jit(solution)/shard_map/reduce_scatter | solution.py:210
  539.3 31.2 %reduce-scatter.23.cloned.1.call-done = bf16[256,1024]{1,0:T(8,128)(2,1)} async-done(((bf16[1024,1024]{1,0:T(8,128)(2,1)}), bf16[256,1024]{1,0:T(8,128)(2,1)}) %reduce-scatter.23.cloned.1.call-update) | async-done | bytes 524304 | tf_op jit(solution)/shard_map/reduce_scatter | solution.py:182
  570.5 34.0 %reduce-scatter.27.cloned.1.call-done = bf16[256,1024]{1,0:T(8,128)(2,1)} async-done(((bf16[1024,1024]{1,0:T(8,128)(2,1)}), bf16[256,1024]{1,0:T(8,128)(2,1)}) %reduce-scatter.27.cloned.1.call-update) | async-done | bytes 524304 | tf_op jit(solution)/shard_map/reduce_scatter | solution.py:182
  643.1 14.9 %multiply_reduce_fusion.1 = (f32[4,1024]{1,0:T(4,128)S(1)}, f32[4,1024,1024]{1,2,0:T(8,128)}) fusion(f32[4,1024,1024]{1,2,0:T(8,128)} %copy-done.1, f32[4,1024]{1,0:T(4,128)S(1)} %log_add_fusion.1, pred[1024]{0:T(1024)(128)(4,1)S(1)} %iota_compare_fusion.1, bf16[1024,4,64]{0,2,1:T(8,128)(2,1)S(1)} %bitcast.453, bf16[1024,4,64]{0,2,1:T(8,128)(2,1)S(1)} %bitcast.452), kind=kOutput, calls=%fused_computation.3 | convolution fusion | flops 557838336 | bytes 34636800 | tf_op jit(solution)/shard_map/qhd,khd->hqk/dot_general | solution.py:239
  681.3 15.3 %multiply_reduce_fusion = (f32[4,1024]{1,0:T(4,128)}, f32[4,1024,1024]{1,2,0:T(8,128)}) fusion(f32[4,1024,1024]{1,2,0:T(8,128)} %copy-done, f32[4,1024]{1,0:T(4,128)S(1)} %copy-done.59, pred[1024]{0:T(1024)(128)(4,1)S(1)} %copy-done.64, bf16[1024,4,64]{0,2,1:T(8,128)(2,1)} %bitcast.455, bf16[1024,4,64]{0,2,1:T(8,128)(2,1)S(1)} %bitcast.450), kind=kOutput, calls=%fused_computation.1 | convolution fusion | flops 557838336 | bytes 34636800 | tf_op jit(solution)/shard_map/qhd,khd->hqk/dot_general | solution.py:239
  768.1 31.3 %reduce-scatter.41.cloned.1.call-done = bf16[128,1312]{1,0:T(8,128)(2,1)} async-done(((bf16[1024,1312]{1,0:T(8,128)(2,1)}), bf16[128,1312]{1,0:T(8,128)(2,1)}) %reduce-scatter.41.cloned.1.call-update) | async-done | bytes 335888
  802.4 61.7 %reduce-scatter.39.cloned.1.call-done = bf16[128,256]{1,0:T(8,128)(2,1)} async-done(((bf16[1024,256]{1,0:T(8,128)(2,1)}), bf16[128,256]{1,0:T(8,128)(2,1)}) %reduce-scatter.39.cloned.1.call-update) | async-done | bytes 65552
  865.7 65.6 %reduce-scatter.37.cloned.1.call-done = bf16[128,768]{1,0:T(8,128)(2,1)} async-done(((bf16[1024,768]{1,0:T(8,128)(2,1)}), bf16[128,768]{1,0:T(8,128)(2,1)}) %reduce-scatter.37.cloned.1.call-update) | async-done | bytes 196624
  933.5 30.9 %reduce-scatter.35.cloned.1.call-done = bf16[256,1024]{1,0:T(8,128)(2,1)} async-done(((bf16[1024,1024]{1,0:T(8,128)(2,1)}), bf16[256,1024]{1,0:T(8,128)(2,1)}) %reduce-scatter.35.cloned.1.call-update) | async-done | bytes 524304 | tf_op jit(solution)/shard_map/reduce_scatter | solution.py:264
  964.4 34.0 %reduce-scatter.31.cloned.1.call-done = bf16[256,1024]{1,0:T(8,128)(2,1)} async-done(((bf16[1024,1024]{1,0:T(8,128)(2,1)}), bf16[256,1024]{1,0:T(8,128)(2,1)}) %reduce-scatter.31.cloned.1.call-update) | async-done | bytes 524304 | tf_op jit(solution)/shard_map/reduce_scatter | solution.py:264
  1002.7 21.4 %all-reduce.3 = (bf16[1024]{0:T(1024)(128)(2,1)S(1)}, bf16[1024]{0:T(1024)(128)(2,1)S(1)}) all-reduce(bf16[1024]{0:T(1024)(128)(2,1)S(1)} %add_convert_fusion.6, bf16[1024]{0:T(1024)(128)(2,1)S(1)} %add_convert_fusion.5), channel_id=10, replica_groups=mesh['dp'=8,'mp'=4] {'dp'}, use_global_device_ids=true, to_apply=%region_32.33.clone | all-reduce | flops 2048 | bytes 8192
  (403 shorter events, 317.8 us)
Async XLA Ops:
  7.2 64.0 %all-gather.16.cloned.1.call-start = ((), (), s32[]{:S(2)}) async-start(), calls=%async_computation.13 | async-start | bytes 1769472 | tf_op jit(solution)/shard_map/all_gather | solution.py:54
  9.1 78.5 %all-gather.22.cloned.1.call-start = ((), (), s32[]{:S(2)}) async-start(), calls=%async_computation.18 | async-start | bytes 2621440 | tf_op jit(solution)/shard_map/all_gather | solution.py:146
  36.6 75.8 %all-gather.14.cloned.1.call-start = ((), (), s32[]{:S(2)}) async-start(), calls=%async_computation.12 | async-start | bytes 2621440 | tf_op jit(solution)/shard_map/all_gather | solution.py:146
  37.3 150.8 %reduce-scatter.25.cloned.1.call-start = ((), (), s32[]{:S(2)}) async-start(), calls=%async_computation.19 | async-start | bytes 5242880 | tf_op jit(solution)/shard_map/reduce_scatter | solution.py:167
  140.7 91.7 %reduce-scatter.21.cloned.1.call-start = ((), (), s32[]{:S(2)}) async-start(), calls=%async_computation.14 | async-start | bytes 5242880 | tf_op jit(solution)/shard_map/reduce_scatter | solution.py:167
  163.9 150.2 %all-gather.20.cloned.1.call-start = ((), (), s32[]{:S(2)}) async-start(), calls=%async_computation.16 | async-start | bytes 1511424 | tf_op jit(solution)/shard_map/all_gather | solution.py:77
  164.5 173.4 %all-gather.26.cloned.1.call-start = ((), (), s32[]{:S(2)}) async-start(), calls=%async_computation.22 | async-start | bytes 2621440 | tf_op jit(solution)/shard_map/all_gather | solution.py:198
  167.1 194.9 %all-gather.18.cloned.1.call-start = ((), (), s32[]{:S(2)}) async-start(), calls=%async_computation.15 | async-start | bytes 2621440 | tf_op jit(solution)/shard_map/all_gather | solution.py:176
  236.1 185.6 %all-gather.28.cloned.1.call-start = ((), (), s32[]{:S(2)}) async-start(), calls=%async_computation.23 | async-start | bytes 3022848 | tf_op jit(solution)/shard_map/all_gather | solution.py:92
  236.9 207.7 %all-gather.32.cloned.1.call-start = ((), (), s32[]{:S(2)}) async-start(), calls=%async_computation.27 | async-start | bytes 2621440 | tf_op jit(solution)/shard_map/all_gather | solution.py:198
  237.5 231.3 %all-gather.24.cloned.1.call-start = ((), (), s32[]{:S(2)}) async-start(), calls=%async_computation.20 | async-start | bytes 2621440 | tf_op jit(solution)/shard_map/all_gather | solution.py:176
  274.6 68.4 %collective-permute-start.2 = (bf16[2,512,656]{1,2,0:T(8,128)(2,1)}, bf16[2,512,656]{1,2,0:T(8,128)(2,1)}, u32[]{:S(2)}, u32[]{:S(2)}) collective-permute-start(bf16[2,512,656]{1,2,0:T(8,128)(2,1)} %maximum_select_fusion.1), channel_id=1, source_target_pairs={{0,16},{4,20},{8,24},{12,28},{16,0},{20,4},{24,8},{28,12},{1,17},{... | collective-permute-start | bytes 4030472 | tf_op jit(solution)/shard_map/ppermute | solution.py:68
  342.9 159.7 %reduce-scatter.29.cloned.1.call-start = ((), (), s32[]{:S(2)}) async-start(), calls=%async_computation.24 | async-start | bytes 2621440 | tf_op jit(solution)/shard_map/reduce_scatter | solution.py:210
  429.1 107.6 %reduce-scatter.33.cloned.1.call-start = ((), (), s32[]{:S(2)}) async-start(), calls=%async_computation.28 | async-start | bytes 2621440 | tf_op jit(solution)/shard_map/reduce_scatter | solution.py:210
  489.4 81.1 %reduce-scatter.23.cloned.1.call-start = ((), (), s32[]{:S(2)}) async-start(), calls=%async_computation.17 | async-start | bytes 2621440 | tf_op jit(solution)/shard_map/reduce_scatter | solution.py:182
  494.4 110.1 %reduce-scatter.27.cloned.1.call-start = ((), (), s32[]{:S(2)}) async-start(), calls=%async_computation.21 | async-start | bytes 2621440 | tf_op jit(solution)/shard_map/reduce_scatter | solution.py:182
  499.3 140.2 %all-gather.30.cloned.1.call-start = ((), (), s32[]{:S(2)}) async-start(), calls=%async_computation.25 | async-start | bytes 2621440 | tf_op jit(solution)/shard_map/all_gather | solution.py:221
  609.6 64.7 %all-gather.34.cloned.1.call-start = ((), (), s32[]{:S(2)}) async-start(), calls=%async_computation.29 | async-start | bytes 2621440 | tf_op jit(solution)/shard_map/all_gather | solution.py:221
  610.2 154.9 %reduce-scatter.43.cloned.1.call-start = ((), (), s32[]{:S(2)}) async-start(), calls=%async_computation.34 | async-start | bytes 1769472
  619.0 180.4 %reduce-scatter.41.cloned.1.call-start = ((), (), s32[]{:S(2)}) async-start(), calls=%async_computation.33 | async-start | bytes 3244032
  639.5 224.6 %reduce-scatter.39.cloned.1.call-start = ((), (), s32[]{:S(2)}) async-start(), calls=%async_computation.32 | async-start | bytes 589824
  732.6 198.7 %reduce-scatter.37.cloned.1.call-start = ((), (), s32[]{:S(2)}) async-start(), calls=%async_computation.31 | async-start | bytes 1769472
  755.2 209.2 %reduce-scatter.35.cloned.1.call-start = ((), (), s32[]{:S(2)}) async-start(), calls=%async_computation.30 | async-start | bytes 2621440 | tf_op jit(solution)/shard_map/reduce_scatter | solution.py:264
  760.5 237.9 %reduce-scatter.31.cloned.1.call-start = ((), (), s32[]{:S(2)}) async-start(), calls=%async_computation.26 | async-start | bytes 2621440 | tf_op jit(solution)/shard_map/reduce_scatter | solution.py:264
  (107 other events, 3237.7 us)
Sparse Core Ops, SparseCore 0:
  10.1 50.8 all-gather.15
  63.1 24.4 all-gather.21
  89.7 22.5 all-gather.13
  140.8 44.5 reduce-scatter.24
  187.9 44.4 reduce-scatter.20
  234.3 79.7 all-gather.19
  316.2 21.5 all-gather.25
  339.4 22.5 all-gather.17
  364.1 57.6 all-gather.27
  423.7 20.7 all-gather.31
  446.1 22.5 all-gather.23
  471.1 31.4 reduce-scatter.28
  505.3 31.3 reduce-scatter.32
  539.1 31.4 reduce-scatter.22
  573.1 31.3 reduce-scatter.26
  609.8 22.6 all-gather.29
  633.8 22.5 all-gather.33
  659.7 64.7 reduce-scatter.42
  728.5 70.9 reduce-scatter.40
  803.0 61.0 reduce-scatter.38
  867.5 63.7 reduce-scatter.36
  934.0 30.3 reduce-scatter.34
  966.9 31.4 reduce-scatter.30
